TPU v7x, 512 devices: a whole 4x8x8 slice. The times are simulated.
512 devices in a mesh: doc: 16 (over y, x_hi), seq: 32 (over z, x_lo, core).
Axes of the slice: x: 4 (x_hi: 2, x_lo: 2; x = x_hi * 2 + x_lo), y: 8, z: 8, core: 2. Of those that a mesh axis runs over, the one named last changes fastest.
Arguments:
- enc_query: bfloat16 [16, 4096, 2048], P('doc', 'seq'), may hold values from -40 to 40
- enc_key: bfloat16 [16, 4096, 2048], P('doc', 'seq'), may hold values from -16 to 16
- enc_value: bfloat16 [16, 4096, 2048], P('doc', 'seq'), may hold values from -6 to 6
- sum_query: bfloat16 [16, 512, 2048], P('doc', 'seq'), may hold values from -70 to 70
- doc_len: int32 [16], P('doc'), may hold values from 1024 to 4096, as said below
- w_memory: bfloat16 [2, 2048, 2048], P(None, None, 'doc'), may hold values from -0.26367188 to 0.26367188
Outputs:
- encoder_out: bfloat16 [16, 4096, 2048], P('doc', 'seq')
- summary_out: bfloat16 [16, 512, 2048], P('doc', 'seq')
Inputs may be any that keep to these rules, and one draw needn't show every extreme that they name: `doc_len`: at least one document has all 4096 tokens valid.
All inputs are finite; a program needn't handle non-finite values.
Results may differ from a plain program's by a relative error of at most 0.012.
Values may be sent and summed in bfloat16 or wider, within the bound.
A program may use at most 64 MiB of HBM per device.

v0:
```python
import math
import jax
import jax.numpy as jnp
from jax import lax
from jax.sharding import PartitionSpec as P

HEAD_DIM = 64


def attend_heads(queries, keys_all, values_all, length, head_dim):
    row_count = queries.shape[0]
    feature_width = queries.shape[1]
    head_count = feature_width // head_dim
    block_rows = math.gcd(row_count, 512)
    grouped = queries.reshape(row_count // block_rows, block_rows, head_count, head_dim)
    key_heads = keys_all.reshape(-1, head_count, head_dim)
    value_heads = values_all.reshape(-1, head_count, head_dim)
    key_valid = jnp.arange(key_heads.shape[0]) < length

    def one_block(query_block):
        scores = jnp.einsum(
            "qhd,khd->hqk", query_block, key_heads, preferred_element_type=jnp.float32
        ) * head_dim ** (-0.5)
        scores = jnp.where(key_valid[None, None, :], scores, -1e30)
        row_max = jnp.max(scores, axis=-1, keepdims=True)
        weights = jnp.exp(scores - row_max)
        denominator = jnp.sum(weights, axis=-1)
        weighted = jnp.einsum(
            "hqk,khd->qhd",
            weights.astype(jnp.bfloat16),
            value_heads,
            preferred_element_type=jnp.float32,
        )
        return (weighted / denominator.T[:, :, None]).astype(jnp.bfloat16)

    return lax.map(one_block, grouped).reshape(row_count, feature_width)


def shards(enc_query, enc_key, enc_value, sum_query, doc_len, w_memory):
    head_dim = HEAD_DIM
    length = doc_len[0]
    head_query, head_key, head_value = (
        lax.all_to_all(enc_query[0], "seq", split_axis=1, concat_axis=0, tiled=True),
        lax.all_to_all(enc_key[0], "seq", split_axis=1, concat_axis=0, tiled=True),
        lax.all_to_all(enc_value[0], "seq", split_axis=1, concat_axis=0, tiled=True),
    )
    context = attend_heads(head_query, head_key, head_value, length, head_dim)
    encoder_out = lax.all_to_all(context, "seq", split_axis=0, concat_axis=1, tiled=True)
    made = jnp.einsum(
        "btd,kdc->btkc",
        lax.all_gather(encoder_out[None], "doc", axis=0, tiled=True),
        w_memory,
        preferred_element_type=jnp.float32,
    )
    memory_rows = made.astype(jnp.bfloat16)
    memory_local = lax.all_to_all(
        lax.all_to_all(memory_rows, "doc", split_axis=0, concat_axis=3, tiled=True),
        "seq",
        split_axis=3,
        concat_axis=1,
        tiled=True,
    )
    memory_keys = memory_local[0, :, 0, :]
    memory_values = memory_local[0, :, 1, :]
    summary_heads = lax.all_to_all(sum_query[0], "seq", split_axis=1, concat_axis=0, tiled=True)
    answer = attend_heads(summary_heads, memory_keys, memory_values, length, head_dim)
    summary_out = lax.all_to_all(answer, "seq", split_axis=0, concat_axis=1, tiled=True)
    return (encoder_out[None], summary_out[None])


def solution(mesh):
    in_specs = (
        P("doc", "seq", None),
        P("doc", "seq", None),
        P("doc", "seq", None),
        P("doc", "seq", None),
        P("doc"),
        P(None, None, "doc"),
    )
    out_specs = (P("doc", "seq", None), P("doc", "seq", None))
    return jax.shard_map(shards, mesh=mesh, in_specs=in_specs, out_specs=out_specs, check_vma=False)
```

profile of v0, /device:TPU:1, one launch (start us, length us, event | category | flops | bytes accessed | tf_op | source)
XLA Modules:
  0.0 431.8 jit_solution(14560852746288561887)
XLA Ops:
  9.3 12.9 %all-to-all-start = ((bf16[128,32,64]{0,2,1:T(8,128)(2,1)}), bf16[128,32,64]{0,2,1:T(8,128)(2,1)S(1)}, u32[]{:S(2)}, u32[]{:S(2)}) async-start(bf16[128,32,64]{0,2,1:T(8,128)(2,1)} %bitcast), calls=%async_computation | async-start | bytes 1048576 | tf_op jit(solution)/shard_map/all_to_all | solution.py:43
  24.3 14.7 %all-to-all-done = bf16[128,32,64]{0,2,1:T(8,128)(2,1)S(1)} async-done(((bf16[128,32,64]{0,2,1:T(8,128)(2,1)}), bf16[128,32,64]{0,2,1:T(8,128)(2,1)S(1)}, u32[]{:S(2)}, u32[]{:S(2)}) %all-to-all-start) | async-done | bytes 524320 | tf_op jit(solution)/shard_map/all_to_all | solution.py:43
  38.9 5.1 %all-to-all-start.1 = ((bf16[128,32,64]{0,2,1:T(8,128)(2,1)}), bf16[128,32,64]{0,2,1:T(8,128)(2,1)S(1)}, u32[]{:S(2)}, u32[]{:S(2)}) async-start(bf16[128,32,64]{0,2,1:T(8,128)(2,1)} %bitcast.2), calls=%async_computation.1 | async-start | bytes 1048576 | tf_op jit(solution)/shard_map/all_to_all | solution.py:44
  46.1 15.0 %all-to-all-done.1 = bf16[128,32,64]{0,2,1:T(8,128)(2,1)S(1)} async-done(((bf16[128,32,64]{0,2,1:T(8,128)(2,1)}), bf16[128,32,64]{0,2,1:T(8,128)(2,1)S(1)}, u32[]{:S(2)}, u32[]{:S(2)}) %all-to-all-start.1) | async-done | bytes 524320 | tf_op jit(solution)/shard_map/all_to_all | solution.py:44
  61.1 4.8 %all-to-all-start.2 = ((bf16[128,32,64]{0,2,1:T(8,128)(2,1)}), bf16[128,32,64]{0,2,1:T(8,128)(2,1)S(1)}, u32[]{:S(2)}, u32[]{:S(2)}) async-start(bf16[128,32,64]{0,2,1:T(8,128)(2,1)} %bitcast.4), calls=%async_computation.2 | async-start | bytes 1048576 | tf_op jit(solution)/shard_map/all_to_all | solution.py:45
  68.2 14.8 %all-to-all-done.2 = bf16[128,32,64]{0,2,1:T(8,128)(2,1)S(1)} async-done(((bf16[128,32,64]{0,2,1:T(8,128)(2,1)}), bf16[128,32,64]{0,2,1:T(8,128)(2,1)S(1)}, u32[]{:S(2)}, u32[]{:S(2)}) %all-to-all-start.2) | async-done | bytes 524320 | tf_op jit(solution)/shard_map/all_to_all | solution.py:45
  83.6 60.9 %while.3 = (s32[]{:T(128)}, bf16[8,512,1,64]{1,3,2,0:T(8,128)(2,1)}, bf16[8,512,1,64]{1,3,2,0:T(8,128)(2,1)}, bf16[4096,1,64]{0,2,1:T(8,128)(2,1)S(1)}, bf16[409...) while((s32[]{:T(128)}, bf16[8,512,1,64]{1,3,2,0:T(8,128)(2,1)}, ...), condition=%wide.region_3.4_spmd.clone, body=%wide.region_0.3_spmd.clone.sunk | while | flops 560008192 | bytes 26373200 | solution.py:36
  88.7 2.5 fusion.68
  96.3 2.5 fusion.68
  99.5 2.3 fusion.66
  103.9 2.5 fusion.68
  107.1 2.3 fusion.66
  111.5 2.5 fusion.68
  114.7 2.3 fusion.66
  119.1 2.5 fusion.68
  122.3 2.3 fusion.66
  126.8 2.5 fusion.68
  129.9 2.3 fusion.66
  134.4 2.5 fusion.68
  142.0 2.5 fusion.68
  146.4 20.8 %all_to_all.132 = bf16[32,128,64]{1,2,0:T(8,128)(2,1)S(1)} all-to-all(bf16[32,128,64]{1,2,0:T(8,128)(2,1)S(1)} %copy.51), channel_id=1, replica_groups=mesh['doc'=16,'seq'=32] {'seq'}, dimensions={0} | all-to-all | bytes 1048576 | tf_op jit(solution)/shard_map/all_to_all | solution.py:48
  168.2 137.7 %all-gather.2.cloned.1.call-done = bf16[16,128,2048]{2,1,0:T(8,128)(2,1)} async-done(((bf16[1,128,2048]{2,1,0:T(8,128)(2,1)}), bf16[16,128,2048]{2,1,0:T(8,128)(2,1)}) %all-gather.2.cloned.1.call-update) | async-done | bytes 8388624 | tf_op jit(solution)/shard_map/all_gather | solution.py:51
  305.9 6.8 %fusion.39 = bf16[16,128,2,128]{3,1,2,0:T(8,128)(2,1)} fusion(bf16[16,128,2048]{2,1,0:T(8,128)(2,1)} %all-gather.2.cloned.1.call-done, bf16[2,2048,128]{2,1,0:T(8,128)(2,1)S(1)} %copy-done), kind=kOutput, calls=%fused_computation.31 | convolution fusion | flops 2148007936 | bytes 10485760 | tf_op jit(solution)/shard_map/btd,kdc->btkc/dot_general | solution.py:49
  312.7 4.3 all-to-all-start.4
  318.1 25.2 %all-to-all-done.4 = bf16[16,128,2,128]{3,1,2,0:T(8,128)(2,1)S(1)} async-done(((bf16[16,128,2,128]{3,1,2,0:T(8,128)(2,1)}), bf16[16,128,2,128]{3,1,2,0:T(8,128)(2,1)S(1)}, u32[]{:S(2)}, u32[]{:S(2)}) %all-to-all-start.4) | async-done | bytes 1048608 | tf_op jit(solution)/shard_map/all_to_all | solution.py:57
  343.3 13.0 %all-to-all-start.6 = ((bf16[32,2,512]{2,1,0:T(2,128)(2,1)}), bf16[32,2,512]{2,1,0:T(2,128)(2,1)S(1)}, u32[]{:S(2)}, u32[]{:S(2)}) async-start(bf16[32,2,512]{2,1,0:T(2,128)(2,1)} %reshape.128), calls=%async_computation.6 | async-start | bytes 131072 | tf_op jit(solution)/shard_map/all_to_all | solution.py:65
  357.0 9.5 %copy.54 = bf16[1,128,2,2048]{1,2,0,3:T(2,128)(2,1)} copy(bf16[1,128,2,2048]{1,3,2,0:T(8,128)(2,1)S(1)} %bitcast.112) | data formatting | bytes 2097152 | tf_op jit(solution)/shard_map/all_to_all | solution.py:57
  366.5 8.3 %all-to-all-start.5 = ((bf16[1,128,2,2048]{1,2,0,3:T(2,128)(2,1)}), bf16[1,128,2,2048]{1,2,0,3:T(2,128)(2,1)S(1)}, u32[]{:S(2)}, u32[]{:S(2)}) async-start(bf16[1,128,2,2048]{1,2,0,3:T(2,128)(2,1)} %copy.54), calls=%async_computation.5 | async-start | bytes 2097152 | tf_op jit(solution)/shard_map/all_to_all | solution.py:56
  375.6 27.1 %all-to-all-done.5 = bf16[1,128,2,2048]{1,2,0,3:T(2,128)(2,1)S(1)} async-done(((bf16[1,128,2,2048]{1,2,0,3:T(2,128)(2,1)}), bf16[1,128,2,2048]{1,2,0,3:T(2,128)(2,1)S(1)}, u32[]{:S(2)}, u32[]{:S(2)}) %all-to-all-start.5) | async-done | bytes 1048608 | tf_op jit(solution)/shard_map/all_to_all | solution.py:56
  403.1 3.4 fusion.33
  406.5 2.7 fusion.34
  411.3 12.6 %all_to_all.133 = bf16[32,2,512]{2,1,0:T(2,128)(2,1)S(1)} all-to-all(bf16[32,2,512]{2,1,0:T(2,128)(2,1)S(1)} %reshape.130), channel_id=1, replica_groups=mesh['doc'=16,'seq'=32] {'seq'}, dimensions={0} | all-to-all | bytes 131072 | tf_op jit(solution)/shard_map/all_to_all | solution.py:67
  (55 shorter events, 46.4 us)
Async XLA Ops:
  7.2 298.8 %copy-start = (bf16[2,2048,128]{2,1,0:T(8,128)(2,1)S(1)}, bf16[2,2048,128]{2,1,0:T(8,128)(2,1)}, u32[]{:S(2)}) copy-start(bf16[2,2048,128]{2,1,0:T(8,128)(2,1)} %param.13) | copy-start | bytes 3145732
  9.3 29.6 %all-to-all-start = ((bf16[128,32,64]{0,2,1:T(8,128)(2,1)}), bf16[128,32,64]{0,2,1:T(8,128)(2,1)S(1)}, u32[]{:S(2)}, u32[]{:S(2)}) async-start(bf16[128,32,64]{0,2,1:T(8,128)(2,1)} %bitcast), calls=%async_computation | async-start | bytes 1048576 | tf_op jit(solution)/shard_map/all_to_all | solution.py:43
  38.9 22.2 %all-to-all-start.1 = ((bf16[128,32,64]{0,2,1:T(8,128)(2,1)}), bf16[128,32,64]{0,2,1:T(8,128)(2,1)S(1)}, u32[]{:S(2)}, u32[]{:S(2)}) async-start(bf16[128,32,64]{0,2,1:T(8,128)(2,1)} %bitcast.2), calls=%async_computation.1 | async-start | bytes 1048576 | tf_op jit(solution)/shard_map/all_to_all | solution.py:44
  61.1 21.9 %all-to-all-start.2 = ((bf16[128,32,64]{0,2,1:T(8,128)(2,1)}), bf16[128,32,64]{0,2,1:T(8,128)(2,1)S(1)}, u32[]{:S(2)}, u32[]{:S(2)}) async-start(bf16[128,32,64]{0,2,1:T(8,128)(2,1)} %bitcast.4), calls=%async_computation.2 | async-start | bytes 1048576 | tf_op jit(solution)/shard_map/all_to_all | solution.py:45
  66.0 240.0 %all-gather.2.cloned.1.call-start = ((), (), s32[]{:S(2)}) async-start(), calls=%async_computation.8 | async-start | bytes 8912896 | tf_op jit(solution)/shard_map/all_gather | solution.py:51
  168.2 148.8 %copy-start.1 = (bf16[1,16,2048]{2,1,0:T(8,128)(2,1)S(1)}, bf16[1,16,2048]{2,1,0:T(8,128)(2,1)}, u32[]{:S(2)}) copy-start(bf16[1,16,2048]{2,1,0:T(8,128)(2,1)} %param.11) | copy-start | bytes 196612
  312.7 30.6 %all-to-all-start.4 = ((bf16[16,128,2,128]{3,1,2,0:T(8,128)(2,1)}), bf16[16,128,2,128]{3,1,2,0:T(8,128)(2,1)S(1)}, u32[]{:S(2)}, u32[]{:S(2)}) async-start(bf16[16,128,2,128]{3,1,2,0:T(8,128)(2,1)} %fusion.39), calls=%async_computation.4 | async-start | bytes 2097152 | tf_op jit(solution)/shard_map/all_to_all | solution.py:57
  343.3 23.1 %all-to-all-start.6 = ((bf16[32,2,512]{2,1,0:T(2,128)(2,1)}), bf16[32,2,512]{2,1,0:T(2,128)(2,1)S(1)}, u32[]{:S(2)}, u32[]{:S(2)}) async-start(bf16[32,2,512]{2,1,0:T(2,128)(2,1)} %reshape.128), calls=%async_computation.6 | async-start | bytes 131072 | tf_op jit(solution)/shard_map/all_to_all | solution.py:65
  366.5 36.2 %all-to-all-start.5 = ((bf16[1,128,2,2048]{1,2,0,3:T(2,128)(2,1)}), bf16[1,128,2,2048]{1,2,0,3:T(2,128)(2,1)S(1)}, u32[]{:S(2)}, u32[]{:S(2)}) async-start(bf16[1,128,2,2048]{1,2,0,3:T(2,128)(2,1)} %copy.54), calls=%async_computation.5 | async-start | bytes 2097152 | tf_op jit(solution)/shard_map/all_to_all | solution.py:56
Sparse Core Ops, SparseCore 0:
  168.3 137.5 all-gather.1
where the time goes:
time: 433 us; the launch traced here: 432 us
  waiting for transfers between devices  235 us (54%)
  matrix products  50.5 us (12%)
  starting transfers between devices  48.4 us (11%)
  blocking collectives  33.4 us (8%)
  other arithmetic  25.1 us (6%)
  local copies, waits for them, and re-layouts  24.8 us (6%)
  between operations  14.9 us (3%)
    all_gather x1, waiting for transfers between devices, shards(): lax.all_gather(encoder_out[None], 'doc', axis=0, tiled=True)  138 us
    all_to_all x1, waiting for transfers between devices, shards(): lax.all_to_all(lax.all_to_all(memory_rows, 'doc', split_axis=0, concat_ax...  27.1 us
    all_to_all x1, waiting for transfers between devices, shards(): lax.all_to_all(memory_rows, 'doc', split_axis=0, concat_axis=3, tiled=True)  25.2 us
    dot_general x9, matrix products, one_block(): jnp.einsum('hqk,khd->qhd', weights.astype(jnp.bfloat16), value_heads, pre...  22.1 us
    dot_general x9, matrix products, one_block(): jnp.einsum('qhd,khd->hqk', query_block, key_heads, preferred_element_type...  21.5 us
    all_to_all x1, blocking collectives, shards(): lax.all_to_all(context, 'seq', split_axis=0, concat_axis=1, tiled=True)  20.8 us
    reduce_sum x9, other arithmetic, one_block(): denominator = jnp.sum(weights, axis=-1)  19.9 us
    all_to_all x1, waiting for transfers between devices, shards(): lax.all_to_all(enc_key[0], 'seq', split_axis=1, concat_axis=0, tiled=True)  15 us
  transfers between devices with their start and end apart: 7, of which 6 were waited for; matrix products, arithmetic and copies ran while one was open for 4% of the time, Pallas kernels for 0%

commit v1 on v0

--- a/solution.py
+++ b/solution.py
@@ -3,6 +3,7 @@
 import jax.numpy as jnp
 from jax import lax
 from jax.sharding import PartitionSpec as P
+from jax.lax import all_to_all, axis_size
 
 HEAD_DIM = 64
 
@@ -48,7 +49,15 @@
     encoder_out = lax.all_to_all(context, "seq", split_axis=0, concat_axis=1, tiled=True)
     made = jnp.einsum(
         "btd,kdc->btkc",
-        lax.all_gather(encoder_out[None], "doc", axis=0, tiled=True),
+        jnp.concatenate(
+            all_to_all(
+                jnp.stack([encoder_out[None]] * axis_size("doc"), axis=0),
+                axis_name="doc",
+                split_axis=0,
+                concat_axis=0,
+            ),
+            axis=0,
+        ),
         w_memory,
         preferred_element_type=jnp.float32,
     )

time: 433 us -> 465 us (1.074)
  blocking collectives: 33.4 us -> 215 us
  waiting for transfers between devices: 235 us -> 108 us
  between operations: 14.9 us -> 1.51 us
    all_to_all x1, blocking collectives: 12.6 us -> 194 us  [shards(): all_to_all(jnp.stack([encoder_out[None]] * axis_size('doc'), axis=0), axi...]
    all_gather x1 -> x0, waiting for transfers between devices: 138 us -> none  [shards(): lax.all_gather(encoder_out[None], 'doc', axis=0, tiled=True)]
    all_to_all x0 -> x1, waiting for transfers between devices: none -> 7.42 us  [shards(): lax.all_to_all(answer, 'seq', split_axis=0, concat_axis=1, tiled=True)]
    all_to_all x2, local copies, waits for them, and re-layouts: 10.2 us -> 4.92 us  [shards(): lax.all_to_all(memory_rows, 'doc', split_axis=0, concat_axis=3, tiled=True)]
    all_to_all x0 -> x1, starting transfers between devices: none -> 4.71 us  [shards(): lax.all_to_all(answer, 'seq', split_axis=0, concat_axis=1, tiled=True)]
  transfers between devices with their start and end apart: 7 -> 7, of which waited for: 6 -> 7; matrix products, arithmetic and copies ran while one was open for 4% -> 3% of each run, Pallas kernels for 0% -> 0%
where the time goes in v1:
time: 465 us; the launch traced here: 464 us
  blocking collectives  215 us (46%)
  waiting for transfers between devices  108 us (23%)
  matrix products  47.1 us (10%)
  starting transfers between devices  46.5 us (10%)
  other arithmetic  25.1 us (5%)
  local copies, waits for them, and re-layouts  21.4 us (5%)
    all_to_all x1, blocking collectives, shards(): all_to_all(jnp.stack([encoder_out[None]] * axis_size('doc'), axis=0), axi...  194 us
    all_to_all x1, waiting for transfers between devices, shards(): lax.all_to_all(lax.all_to_all(memory_rows, 'doc', split_axis=0, concat_ax...  27.3 us
    all_to_all x1, waiting for transfers between devices, shards(): lax.all_to_all(memory_rows, 'doc', split_axis=0, concat_axis=3, tiled=True)  24.9 us
    dot_general x9, matrix products, one_block(): jnp.einsum('hqk,khd->qhd', weights.astype(jnp.bfloat16), value_heads, pre...  22.1 us
    dot_general x9, matrix products, one_block(): jnp.einsum('qhd,khd->hqk', query_block, key_heads, preferred_element_type...  21.6 us
    all_to_all x1, blocking collectives, shards(): lax.all_to_all(context, 'seq', split_axis=0, concat_axis=1, tiled=True)  20.7 us
    reduce_sum x9, other arithmetic, one_block(): denominator = jnp.sum(weights, axis=-1)  19.9 us
    all_to_all x1, waiting for transfers between devices, shards(): lax.all_to_all(enc_key[0], 'seq', split_axis=1, concat_axis=0, tiled=True)  15 us
  transfers between devices with their start and end apart: 7, of which 7 were waited for; matrix products, arithmetic and copies ran while one was open for 3% of the time, Pallas kernels for 0%

profile of v1, /device:TPU:1, one launch (start us, length us, event | category | flops | bytes accessed | tf_op | source)
XLA Modules:
  0.0 464.0 jit_solution(15954675010087482746)
XLA Ops:
  2.8 12.9 %all-to-all-start = ((bf16[128,32,64]{0,2,1:T(8,128)(2,1)}), bf16[128,32,64]{0,2,1:T(8,128)(2,1)S(1)}, u32[]{:S(2)}, u32[]{:S(2)}) async-start(bf16[128,32,64]{0,2,1:T(8,128)(2,1)} %bitcast), calls=%async_computation | async-start | bytes 1048576 | tf_op jit(solution)/shard_map/all_to_all | solution.py:44
  17.7 14.7 %all-to-all-done = bf16[128,32,64]{0,2,1:T(8,128)(2,1)S(1)} async-done(((bf16[128,32,64]{0,2,1:T(8,128)(2,1)}), bf16[128,32,64]{0,2,1:T(8,128)(2,1)S(1)}, u32[]{:S(2)}, u32[]{:S(2)}) %all-to-all-start) | async-done | bytes 524320 | tf_op jit(solution)/shard_map/all_to_all | solution.py:44
  32.4 5.1 %all-to-all-start.1 = ((bf16[128,32,64]{0,2,1:T(8,128)(2,1)}), bf16[128,32,64]{0,2,1:T(8,128)(2,1)S(1)}, u32[]{:S(2)}, u32[]{:S(2)}) async-start(bf16[128,32,64]{0,2,1:T(8,128)(2,1)} %bitcast.2), calls=%async_computation.1 | async-start | bytes 1048576 | tf_op jit(solution)/shard_map/all_to_all | solution.py:45
  39.5 15.0 %all-to-all-done.1 = bf16[128,32,64]{0,2,1:T(8,128)(2,1)S(1)} async-done(((bf16[128,32,64]{0,2,1:T(8,128)(2,1)}), bf16[128,32,64]{0,2,1:T(8,128)(2,1)S(1)}, u32[]{:S(2)}, u32[]{:S(2)}) %all-to-all-start.1) | async-done | bytes 524320 | tf_op jit(solution)/shard_map/all_to_all | solution.py:45
  54.6 4.8 %all-to-all-start.2 = ((bf16[128,32,64]{0,2,1:T(8,128)(2,1)}), bf16[128,32,64]{0,2,1:T(8,128)(2,1)S(1)}, u32[]{:S(2)}, u32[]{:S(2)}) async-start(bf16[128,32,64]{0,2,1:T(8,128)(2,1)} %bitcast.4), calls=%async_computation.2 | async-start | bytes 1048576 | tf_op jit(solution)/shard_map/all_to_all | solution.py:46
  61.6 14.9 %all-to-all-done.2 = bf16[128,32,64]{0,2,1:T(8,128)(2,1)S(1)} async-done(((bf16[128,32,64]{0,2,1:T(8,128)(2,1)}), bf16[128,32,64]{0,2,1:T(8,128)(2,1)S(1)}, u32[]{:S(2)}, u32[]{:S(2)}) %all-to-all-start.2) | async-done | bytes 524320 | tf_op jit(solution)/shard_map/all_to_all | solution.py:46
  77.1 60.9 %while.3 = (s32[]{:T(128)}, bf16[8,512,1,64]{1,3,2,0:T(8,128)(2,1)}, bf16[8,512,1,64]{1,3,2,0:T(8,128)(2,1)}, bf16[4096,1,64]{0,2,1:T(8,128)(2,1)S(1)}, bf16[409...) while((s32[]{:T(128)}, bf16[8,512,1,64]{1,3,2,0:T(8,128)(2,1)}, ...), condition=%wide.region_3.4_spmd.clone, body=%wide.region_0.3_spmd.clone.sunk | while | flops 560008192 | bytes 26373200 | solution.py:37
  82.2 2.5 fusion.68
  85.3 2.3 fusion.66
  89.8 2.5 fusion.68
  97.4 2.5 fusion.68
  105.0 2.5 fusion.68
  108.2 2.3 fusion.66
  112.6 2.5 fusion.68
  120.2 2.5 fusion.68
  127.8 2.5 fusion.68
  131.0 2.3 fusion.66
  135.4 2.5 fusion.68
  139.9 20.7 %all_to_all.137 = bf16[32,128,64]{1,2,0:T(8,128)(2,1)S(1)} all-to-all(bf16[32,128,64]{1,2,0:T(8,128)(2,1)S(1)} %copy.53), channel_id=1, replica_groups=mesh['doc'=16,'seq'=32] {'seq'}, dimensions={0} | all-to-all | bytes 1048576 | tf_op jit(solution)/shard_map/all_to_all | solution.py:49
  161.9 193.9 %all_to_all.138 = bf16[16,1,128,2048]{3,2,1,0:T(8,128)(2,1)S(1)} all-to-all(bf16[16,1,128,2048]{3,2,1,0:T(8,128)(2,1)S(1)} %stack.3), channel_id=1, replica_groups=mesh['doc'=16,'seq'=32] {'doc'}, dimensions={0} | all-to-all | bytes 16777216 | tf_op jit(solution)/shard_map/all_to_all | solution.py:53
  355.8 3.4 fusion.39
  359.2 4.3 all-to-all-start.5
  364.5 24.9 %all-to-all-done.5 = bf16[16,128,2,128]{3,1,2,0:T(8,128)(2,1)S(1)} async-done(((bf16[16,128,2,128]{3,1,2,0:T(8,128)(2,1)}), bf16[16,128,2,128]{3,1,2,0:T(8,128)(2,1)S(1)}, u32[]{:S(2)}, u32[]{:S(2)}) %all-to-all-start.5) | async-done | bytes 1048608 | tf_op jit(solution)/shard_map/all_to_all | solution.py:66
  389.4 9.8 %all-to-all-start.7 = ((bf16[32,2,512]{2,1,0:T(2,128)(2,1)}), bf16[32,2,512]{2,1,0:T(2,128)(2,1)S(1)}, u32[]{:S(2)}, u32[]{:S(2)}) async-start(bf16[32,2,512]{2,1,0:T(2,128)(2,1)} %reshape.137), calls=%async_computation.7 | async-start | bytes 131072 | tf_op jit(solution)/shard_map/all_to_all | solution.py:74
  400.5 3.6 copy.56
  404.2 3.4 all-to-all-done.7
  407.6 4.9 %all-to-all-start.6 = ((bf16[1,128,2,2048]{1,2,0,3:T(2,128)(2,1)}), bf16[1,128,2,2048]{1,2,0,3:T(2,128)(2,1)S(1)}, u32[]{:S(2)}, u32[]{:S(2)}) async-start(bf16[1,128,2,2048]{1,2,0,3:T(2,128)(2,1)} %copy.56), calls=%async_computation.6 | async-start | bytes 2097152 | tf_op jit(solution)/shard_map/all_to_all | solution.py:65
  413.2 27.3 %all-to-all-done.6 = bf16[1,128,2,2048]{1,2,0,3:T(2,128)(2,1)S(1)} async-done(((bf16[1,128,2,2048]{1,2,0,3:T(2,128)(2,1)}), bf16[1,128,2,2048]{1,2,0,3:T(2,128)(2,1)S(1)}, u32[]{:S(2)}, u32[]{:S(2)}) %all-to-all-start.6) | async-done | bytes 1048608 | tf_op jit(solution)/shard_map/all_to_all | solution.py:65
  441.0 3.4 fusion.33
  444.4 2.7 fusion.34
  449.9 4.7 %all-to-all-start.8 = ((bf16[32,2,512]{2,1,0:T(2,128)(2,1)}), bf16[32,2,512]{2,1,0:T(2,128)(2,1)S(1)}, u32[]{:S(2)}, u32[]{:S(2)}) async-start(bf16[32,2,512]{2,1,0:T(2,128)(2,1)} %reshape.139), calls=%async_computation.8 | async-start | bytes 131072 | tf_op jit(solution)/shard_map/all_to_all | solution.py:76
  455.6 7.4 %all-to-all-done.8 = bf16[32,2,512]{2,1,0:T(2,128)(2,1)S(1)} async-done(((bf16[32,2,512]{2,1,0:T(2,128)(2,1)}), bf16[32,2,512]{2,1,0:T(2,128)(2,1)S(1)}, u32[]{:S(2)}, u32[]{:S(2)}) %all-to-all-start.8) | async-done | bytes 65568 | tf_op jit(solution)/shard_map/all_to_all | solution.py:76
  (56 shorter events, 53.4 us)
Async XLA Ops:
  0.6 355.1 %copy-start = (bf16[2,2048,128]{2,1,0:T(8,128)(2,1)S(1)}, bf16[2,2048,128]{2,1,0:T(8,128)(2,1)}, u32[]{:S(2)}) copy-start(bf16[2,2048,128]{2,1,0:T(8,128)(2,1)} %param.13) | copy-start | bytes 3145732
  2.8 29.6 %all-to-all-start = ((bf16[128,32,64]{0,2,1:T(8,128)(2,1)}), bf16[128,32,64]{0,2,1:T(8,128)(2,1)S(1)}, u32[]{:S(2)}, u32[]{:S(2)}) async-start(bf16[128,32,64]{0,2,1:T(8,128)(2,1)} %bitcast), calls=%async_computation | async-start | bytes 1048576 | tf_op jit(solution)/shard_map/all_to_all | solution.py:44
  32.4 22.2 %all-to-all-start.1 = ((bf16[128,32,64]{0,2,1:T(8,128)(2,1)}), bf16[128,32,64]{0,2,1:T(8,128)(2,1)S(1)}, u32[]{:S(2)}, u32[]{:S(2)}) async-start(bf16[128,32,64]{0,2,1:T(8,128)(2,1)} %bitcast.2), calls=%async_computation.1 | async-start | bytes 1048576 | tf_op jit(solution)/shard_map/all_to_all | solution.py:45
  54.6 21.9 %all-to-all-start.2 = ((bf16[128,32,64]{0,2,1:T(8,128)(2,1)}), bf16[128,32,64]{0,2,1:T(8,128)(2,1)S(1)}, u32[]{:S(2)}, u32[]{:S(2)}) async-start(bf16[128,32,64]{0,2,1:T(8,128)(2,1)} %bitcast.4), calls=%async_computation.2 | async-start | bytes 1048576 | tf_op jit(solution)/shard_map/all_to_all | solution.py:46
  355.8 7.7 %copy-start.1 = (bf16[1,16,2048]{2,1,0:T(8,128)(2,1)S(1)}, bf16[1,16,2048]{2,1,0:T(8,128)(2,1)}, u32[]{:S(2)}) copy-start(bf16[1,16,2048]{2,1,0:T(8,128)(2,1)} %param.11) | copy-start | bytes 196612
  359.2 30.2 %all-to-all-start.5 = ((bf16[16,128,2,128]{3,1,2,0:T(8,128)(2,1)}), bf16[16,128,2,128]{3,1,2,0:T(8,128)(2,1)S(1)}, u32[]{:S(2)}, u32[]{:S(2)}) async-start(bf16[16,128,2,128]{3,1,2,0:T(8,128)(2,1)} %fusion.39), calls=%async_computation.5 | async-start | bytes 2097152 | tf_op jit(solution)/shard_map/all_to_all | solution.py:66
  389.4 18.1 %all-to-all-start.7 = ((bf16[32,2,512]{2,1,0:T(2,128)(2,1)}), bf16[32,2,512]{2,1,0:T(2,128)(2,1)S(1)}, u32[]{:S(2)}, u32[]{:S(2)}) async-start(bf16[32,2,512]{2,1,0:T(2,128)(2,1)} %reshape.137), calls=%async_computation.7 | async-start | bytes 131072 | tf_op jit(solution)/shard_map/all_to_all | solution.py:74
  407.6 33.0 %all-to-all-start.6 = ((bf16[1,128,2,2048]{1,2,0,3:T(2,128)(2,1)}), bf16[1,128,2,2048]{1,2,0,3:T(2,128)(2,1)S(1)}, u32[]{:S(2)}, u32[]{:S(2)}) async-start(bf16[1,128,2,2048]{1,2,0,3:T(2,128)(2,1)} %copy.56), calls=%async_computation.6 | async-start | bytes 2097152 | tf_op jit(solution)/shard_map/all_to_all | solution.py:65
  449.9 13.1 %all-to-all-start.8 = ((bf16[32,2,512]{2,1,0:T(2,128)(2,1)}), bf16[32,2,512]{2,1,0:T(2,128)(2,1)S(1)}, u32[]{:S(2)}, u32[]{:S(2)}) async-start(bf16[32,2,512]{2,1,0:T(2,128)(2,1)} %reshape.139), calls=%async_computation.8 | async-start | bytes 131072 | tf_op jit(solution)/shard_map/all_to_all | solution.py:76
